TPU v7x, 32 devices: a whole 2x2x4 slice. The times are simulated.
32 devices in a mesh: guide: 2 (over core), tensor: 2 (over y), batch: 8 (over z, x).
Axes of the slice: x: 2, y: 2, z: 4, core: 2. Of those that a mesh axis runs over, the one named last changes fastest.
Arguments:
- latents: float32 [8, 16, 448], P('batch'), may hold values from -6 to 6
- lengths: int32 [8], P('batch'), may hold values from 1 to 448, 2240 in all
- timesteps: int32 [8], P('batch'), may hold values from 100 to 599
- guidance: float32 [8], P('batch'), may hold values from 1.5 to 6
- condition: float32 [2, 8, 1152], P('guide', 'batch'), may hold values from -6 to 6
- embed_weight: float32 [16, 1152], replicated, may hold values from -1.5 to 1.5
- modulation_weight: bfloat16 [2, 1152, 6, 1152], P(None, 'batch', None, 'tensor'), may hold values from -0.1875 to 0.1875
- final_modulation: bfloat16 [1152, 2, 1152], P('batch', None, 'tensor'), may hold values from -0.1875 to 0.1875
- qkv_weight: bfloat16 [2, 1152, 3, 1152], P(None, 'batch', None, 'tensor'), may hold values from -15 to 15
- proj_weight: bfloat16 [2, 1152, 1152], P(None, 'tensor', 'batch'), may hold values from -0.1875 to 0.1875
- up_weight: bfloat16 [2, 1152, 4608], P(None, 'batch', 'tensor'), may hold values from -0.1875 to 0.1875
- down_weight: bfloat16 [2, 4608, 1152], P(None, 'tensor', 'batch'), may hold values from -0.09375 to 0.09375
- output_weight: bfloat16 [1152, 16], replicated, may hold values from -0.1875 to 0.1875
Outputs:
- guided_noise: float32 [8, 16, 448], P('batch', 'guide', 'tensor')
- previous_latents: float32 [8, 16, 448], P('batch', 'guide', 'tensor')
Inputs may be any that keep to these rules, and one draw needn't show every extreme that they name: `lengths`: at least one request has exactly 448 live tokens; all requests together have 8 * 448 * 5 // 8.
All inputs are finite; a program needn't handle non-finite values. No bound on the sum of `lengths` on one device may be relied on, other than what follows from the above.
Results may differ from a plain program's by a relative error of at most 0.025.
Values may be sent and summed in bfloat16 or wider, within the bound.
No kernel may reach another device: no remote copies, remote signals or barrier semaphores. Data moves between devices by JAX's collectives and lax.ppermute only.
A program may use at most 128 MiB of HBM per device.

v0:
```python
import math
import jax
import jax.numpy as jnp
from jax import lax
from jax.sharding import PartitionSpec as P

HDIM = 72
TRAIN_STEPS = 1000
STRIDE = 20
norm_epsilon = 1e-06


def from_partner(block, axis, distance):
    count = lax.axis_size(axis)
    route = []
    for low in range(count):
        high = low | 1 << distance
        if high != low and high < count:
            route += [(low, high), (high, low)]
    return lax.ppermute(block, axis, route)


def layer_norm(values):
    center = values - jnp.mean(values, axis=-1, keepdims=True)
    spread = jnp.mean(center * center, axis=-1, keepdims=True)
    return center * lax.rsqrt(spread + norm_epsilon)


def modulate(values, shift, scale):
    return layer_norm(values) * (1.0 + scale[:, None, :]) + shift[:, None, :]


def position_table(row_count, width):
    rows_at = jnp.arange(row_count, dtype=jnp.int32).astype(jnp.float32)
    half_width = width // 2
    frequency = jnp.exp(
        jnp.arange(half_width, dtype=jnp.float32) * (-math.log(10000.0) / half_width)
    )
    angles = rows_at[:, None] * frequency[None, :]
    return jnp.concatenate([jnp.sin(angles), jnp.cos(angles)], axis=1)


def attend(operands):
    projected_item, key_live = operands
    score_scale = 1.0 / math.sqrt(HDIM)
    scores = (
        jnp.einsum(
            "qhd,khd->hqk",
            projected_item[:, 0],
            projected_item[:, 1],
            preferred_element_type=jnp.float32,
        )
        * score_scale
    )
    scores = jnp.where(key_live[None, None, :], scores, -jnp.inf)
    row_max = jnp.max(scores, axis=-1, keepdims=True)
    exp_scores = jnp.exp(scores - row_max)
    probabilities = (exp_scores / jnp.sum(exp_scores, axis=-1, keepdims=True)).astype(jnp.bfloat16)
    attended = jnp.einsum(
        "hqk,khd->qhd", probabilities, projected_item[:, 2], preferred_element_type=jnp.float32
    )
    return attended.astype(jnp.bfloat16).reshape(
        attended.shape[0], attended.shape[1] * attended.shape[2]
    )


def local(
    latents,
    lengths,
    timesteps,
    guidance,
    condition,
    embed_weight,
    modulation_weight,
    final_modulation,
    qkv_weight,
    proj_weight,
    up_weight,
    down_weight,
    output_weight,
):
    tensor_count = lax.axis_size("tensor")
    batch_count = lax.axis_size("batch")
    tensor_at = lax.axis_index("tensor")
    batch_at = lax.axis_index("batch")
    guide_at = lax.axis_index("guide")
    req_local, patch_size, max_len = latents.shape
    width = embed_weight.shape[1]
    layer_count = qkv_weight.shape[0]
    head_cols = qkv_weight.shape[3]
    heads_local = head_cols // HDIM
    rows_local = max_len // tensor_count
    width_piece = width // batch_count
    mod_count = 6 * layer_count + 2
    is_first = guide_at == 0

    def rows_product(activation, shard):
        return jnp.dot(
            activation,
            lax.all_gather(shard, "batch", axis=0, tiled=True),
            preferred_element_type=jnp.float32,
        )

    def cols_product(activation, shard):
        return jnp.dot(
            activation,
            lax.all_gather(shard, "batch", axis=1, tiled=True),
            preferred_element_type=jnp.float32,
        )

    cond_act = jax.nn.silu(condition[0]).astype(jnp.bfloat16)
    cond_all = lax.all_gather(cond_act, "batch", axis=0, tiled=True)
    cond_cols = lax.dynamic_slice_in_dim(cond_all, batch_at * width_piece, width_piece, 1)
    block_local = jnp.transpose(modulation_weight, (1, 0, 2, 3)).reshape(
        width_piece, 6 * layer_count * head_cols
    )
    mod_local = jnp.concatenate(
        [block_local, final_modulation.reshape(width_piece, 2 * head_cols)], axis=1
    )
    mod_mine = lax.psum_scatter(
        jnp.dot(cond_cols, mod_local, preferred_element_type=jnp.float32),
        "batch",
        scatter_dimension=0,
        tiled=True,
    )
    mod_full = lax.all_gather(
        mod_mine.reshape(req_local, mod_count, head_cols), "tensor", axis=2, tiled=True
    )
    positions = jnp.arange(max_len, dtype=jnp.int32)
    live_mask = positions[None, :] < lengths[:, None]
    own_start = tensor_at * rows_local
    own_latents = lax.dynamic_slice_in_dim(latents, own_start, rows_local, 2)
    own_live = lax.dynamic_slice_in_dim(live_mask, own_start, rows_local, 1)
    hidden_state = (
        jnp.einsum("rpl,pd->rld", latents, embed_weight, precision=lax.Precision.HIGHEST)
        + position_table(max_len, width)[None]
    )
    for layer_at in range(layer_count):
        modulation = mod_full[:, 6 * layer_at : 6 * layer_at + 6]
        normed = modulate(hidden_state, modulation[:, 0], modulation[:, 1]).astype(jnp.bfloat16)
        projected = rows_product(
            normed.reshape(req_local * max_len, width),
            qkv_weight[layer_at].reshape(width_piece, 3 * head_cols),
        ).astype(jnp.bfloat16)
        projected = projected.reshape(req_local, max_len, 3, heads_local, HDIM)
        attended = lax.map(attend, (projected, live_mask))
        branch = cols_product(
            attended.reshape(req_local * max_len, head_cols), proj_weight[layer_at]
        ).reshape(req_local, max_len, width)
        branch = lax.psum(branch.astype(jnp.bfloat16), "tensor").astype(jnp.float32)
        hidden_state = hidden_state + modulation[:, 2][:, None, :] * branch
        normed = modulate(hidden_state, modulation[:, 3], modulation[:, 4]).astype(jnp.bfloat16)
        hidden_units = jax.nn.gelu(
            rows_product(normed.reshape(req_local * max_len, width), up_weight[layer_at]),
            approximate=True,
        ).astype(jnp.bfloat16)
        branch = cols_product(hidden_units, down_weight[layer_at]).reshape(
            req_local, max_len, width
        )
        branch = lax.psum(branch.astype(jnp.bfloat16), "tensor").astype(jnp.float32)
        hidden_state = hidden_state + modulation[:, 5][:, None, :] * branch
    hidden_state = lax.dynamic_slice_in_dim(hidden_state, own_start, rows_local, 1)
    final_in = modulate(
        hidden_state, mod_full[:, 6 * layer_count], mod_full[:, 6 * layer_count + 1]
    ).astype(jnp.bfloat16)
    noise_own = jnp.einsum(
        "rld,dp->rpl", final_in, output_weight, preferred_element_type=jnp.float32
    )
    half_patch = patch_size // 2
    mine_noise = lax.dynamic_slice_in_dim(noise_own, guide_at * half_patch, half_patch, 1)
    other_noise = lax.dynamic_slice_in_dim(noise_own, (1 - guide_at) * half_patch, half_patch, 1)
    partner_noise = from_partner(other_noise, "guide", 0)
    cond_noise = jnp.where(is_first, mine_noise, partner_noise)
    uncond_noise = jnp.where(is_first, partner_noise, mine_noise)
    live_out = own_live[:, None, :]
    guided = uncond_noise + guidance[:, None, None] * (cond_noise - uncond_noise)
    guided = jnp.where(live_out, guided, 0.0)
    half_latents = lax.dynamic_slice_in_dim(own_latents, guide_at * half_patch, half_patch, 1)
    beta_values = jnp.linspace(0.0001, 0.02, TRAIN_STEPS, dtype=jnp.float32)
    alpha_bar = jnp.cumprod(1.0 - beta_values)
    step_ids = jnp.arange(TRAIN_STEPS, dtype=jnp.int32)
    alpha_now = jnp.sum(
        jnp.where(step_ids[None, :] == timesteps[:, None], alpha_bar[None, :], 0.0), axis=1
    )[:, None, None]
    alpha_prev = jnp.sum(
        jnp.where(step_ids[None, :] == (timesteps - STRIDE)[:, None], alpha_bar[None, :], 0.0),
        axis=1,
    )[:, None, None]
    start_est = (half_latents - jnp.sqrt(1.0 - alpha_now) * guided) / jnp.sqrt(alpha_now)
    previous = jnp.sqrt(alpha_prev) * start_est + jnp.sqrt(1.0 - alpha_prev) * guided
    previous = jnp.where(live_out, previous, 0.0)
    return (guided, previous)


def solution(mesh):
    in_specs = (
        P("batch", None, None),
        P("batch"),
        P("batch"),
        P("batch"),
        P("guide", "batch", None),
        P(),
        P(None, "batch", None, "tensor"),
        P("batch", None, "tensor"),
        P(None, "batch", None, "tensor"),
        P(None, "tensor", "batch"),
        P(None, "batch", "tensor"),
        P(None, "tensor", "batch"),
        P(),
    )
    out_specs = (P("batch", "guide", "tensor"), P("batch", "guide", "tensor"))
    return jax.shard_map(local, mesh=mesh, in_specs=in_specs, out_specs=out_specs, check_vma=False)
```

profile of v0, /device:TPU:1, one launch (start us, length us, event | category | flops | bytes accessed | tf_op | source)
XLA Modules:
  0.0 909.3 jit_solution(10363798787262294825)
XLA Ops:
  7.2 0.7 fusion.119
  7.9 25.4 %all-gather.6 = bf16[8,1,1152]{2,1,0:T(2,128)(2,1)S(1)} all-gather(bf16[1,1,1152]{2,1,0:T(2,128)(2,1)S(1)} %fusion.119), channel_id=1, replica_groups=mesh['guide'=2,'tensor'=2,'batch'=8] {'batch'}, dimensions={0}, use_global_device_ids=true | all-gather | bytes 20736 | tf_op jit(solution)/shard_map/all_gather | solution.py:112
  33.3 2.2 copy.40
  35.6 3.2 reshape.338
  39.2 2.7 fusion.58
  42.3 1.3 reshape_squeeze.6
  43.8 0.8 fusion.144
  44.6 4.1 multiply_sine_fusion
  48.7 2.1 fusion.145
  52.5 64.8 %all-reduce.16.cloned.1.call-done = f32[8,8064]{1,0:T(8,128)} async-done(((f32[8,8064]{1,0:T(8,128)}), f32[8,8064]{1,0:T(8,128)}) %all-reduce.16.cloned.1.call-update) | async-done | bytes 258064
  117.3 1.7 dynamic-slice_reduce_fusion
  119.2 6.8 all_gather.31
  126.0 62.0 %slice_reduce_fusion.2 = (f32[1152]{0:T(1024)S(1)}, f32[1152]{0:T(1024)S(1)}, f32[1152]{0:T(1024)S(1)}, f32[1152]{0:T(1024)S(1)}, f32[1152]{0:T(1024)S(1)}, /*in...) fusion(f32[1,14,1152]{1,0,2:T(1,128)S(1)} %all_gather.31), kind=kLoop, calls=%fused_computation.104 | loop fusion | flops 5760 | bytes 129024 | tf_op jit(solution)/shard_map/slice | solution.py:161
  188.0 4.9 all-gather.16.cloned.1.call-done
  192.9 5.8 convolution_convert_fusion.1
  198.7 3.0 copy.43
  201.7 5.9 fusion.146
  207.6 3.9 fusion.65
  211.5 26.3 %all-gather.20.cloned.1.call-done = bf16[1,576,1152]{1,2,0:T(8,128)(2,1)} async-done(((bf16[1,576,144]{1,2,0:T(8,128)(2,1)}), bf16[1,576,1152]{1,2,0:T(8,128)(2,1)}) %all-gather.20.cloned.1.call-update) | async-done | bytes 1327120 | tf_op jit(solution)/shard_map/all_gather | solution.py:107
  237.8 3.5 fusion.50
  241.4 1.2 fusion.141
  243.1 1.2 fusion.142
  244.3 35.8 %all-reduce.8.cloned.1.call-done = bf16[1,448,1152]{2,1,0:T(8,128)(2,1)} async-done(((bf16[1,448,1152]{2,1,0:T(8,128)(2,1)}), bf16[1,448,1152]{2,1,0:T(8,128)(2,1)}) %all-reduce.8.cloned.1.call-update) | async-done | bytes 1032208 | tf_op jit(solution)/shard_map/psum | solution.py:150
  280.1 2.2 fusion.140
  282.8 85.9 %all-gather.22.cloned.1.call-done = bf16[1,1152,2304]{2,1,0:T(8,128)(2,1)} async-done(((bf16[1,144,2304]{2,1,0:T(8,128)(2,1)}), bf16[1,1152,2304]{2,1,0:T(8,128)(2,1)}) %all-gather.22.cloned.1.call-update) | async-done | bytes 5308432 | tf_op jit(solution)/shard_map/all_gather | solution.py:100
  368.6 87.5 %all-gather.24.cloned.1.call-done = bf16[1,2304,1152]{1,2,0:T(8,128)(2,1)} async-done(((bf16[1,2304,144]{1,2,0:T(8,128)(2,1)}), bf16[1,2304,1152]{1,2,0:T(8,128)(2,1)}) %all-gather.24.cloned.1.call-update) | async-done | bytes 5308432 | tf_op jit(solution)/shard_map/all_gather | solution.py:107
  456.2 10.9 %fusion.55 = bf16[1,448,1152]{2,1,0:T(8,128)(2,1)} fusion(bf16[1,2304,1152]{1,2,0:T(8,128)(2,1)} %all-gather.24.cloned.1.call-done, bf16[1,1152,2304]{2,1,0:T(8,128)(2,1)} %all-gather.22.cloned.1.call-done, f32[1,448,1152]{2,1,0:T(8,128)S(1)} %get-tuple-element.47, f32[1152]{0:T(1024)S(1)} %get-tuple-element.34, f32[1152]{0:T(1024)S(1)} %get-tuple-element.35, ...), kind=kOutput, calls=%fused_computation.54 | convolution fusion | flops 4768727040 | bytes 13726208 | tf_op jit(solution)/shard_map/dot_general | solution.py:105
  467.5 1.2 reshape_squeeze.7
  469.7 36.3 %all-reduce.10.cloned.1.call-done = bf16[1,448,1152]{2,1,0:T(8,128)(2,1)} async-done(((bf16[1,448,1152]{2,1,0:T(8,128)(2,1)}), bf16[1,448,1152]{2,1,0:T(8,128)(2,1)}) %all-reduce.10.cloned.1.call-update) | async-done | bytes 1032208 | tf_op jit(solution)/shard_map/psum | solution.py:160
  506.0 1.7 fusion.137
  508.2 71.6 %all-gather.18.cloned.1.call-done = bf16[1152,1728]{1,0:T(8,128)(2,1)} async-done(((bf16[144,1728]{1,0:T(8,128)(2,1)}), bf16[1152,1728]{1,0:T(8,128)(2,1)}) %all-gather.18.cloned.1.call-update) | async-done | bytes 3981328 | tf_op jit(solution)/shard_map/all_gather | solution.py:100
  579.8 6.0 convolution_convert_fusion
  585.8 3.7 copy.46
  589.5 7.2 fusion.147
  596.7 4.9 fusion.64
  601.6 23.1 %all-gather.26.cloned.1.call-done = bf16[1,576,1152]{1,2,0:T(8,128)(2,1)} async-done(((bf16[1,576,144]{1,2,0:T(8,128)(2,1)}), bf16[1,576,1152]{1,2,0:T(8,128)(2,1)}) %all-gather.26.cloned.1.call-update) | async-done | bytes 1327120 | tf_op jit(solution)/shard_map/all_gather | solution.py:107
  624.7 3.6 fusion.51
  629.9 37.2 %all-reduce.12.cloned.1.call-done = bf16[1,448,1152]{2,1,0:T(8,128)(2,1)} async-done(((bf16[1,448,1152]{2,1,0:T(8,128)(2,1)}), bf16[1,448,1152]{2,1,0:T(8,128)(2,1)}) %all-reduce.12.cloned.1.call-update) | async-done | bytes 1032208 | tf_op jit(solution)/shard_map/psum | solution.py:150
  667.1 1.8 fusion.139
  669.0 1.3 copy-done.3
  670.6 85.2 %all-gather.28.cloned.1.call-done = bf16[1,1152,2304]{2,1,0:T(8,128)(2,1)} async-done(((bf16[1,144,2304]{2,1,0:T(8,128)(2,1)}), bf16[1,1152,2304]{2,1,0:T(8,128)(2,1)}) %all-gather.28.cloned.1.call-update) | async-done | bytes 5308432 | tf_op jit(solution)/shard_map/all_gather | solution.py:100
  755.8 87.5 %all-gather.30.cloned.1.call-done = bf16[1,2304,1152]{1,2,0:T(8,128)(2,1)} async-done(((bf16[1,2304,144]{1,2,0:T(8,128)(2,1)}), bf16[1,2304,1152]{1,2,0:T(8,128)(2,1)}) %all-gather.30.cloned.1.call-update) | async-done | bytes 5308432 | tf_op jit(solution)/shard_map/all_gather | solution.py:107
  843.4 11.6 %fusion.52 = bf16[1,448,1152]{2,1,0:T(8,128)(2,1)} fusion(bf16[1,2304,1152]{1,2,0:T(8,128)(2,1)} %all-gather.30.cloned.1.call-done, bf16[1,1152,2304]{2,1,0:T(8,128)(2,1)} %all-gather.28.cloned.1.call-done, f32[1,448,1152]{2,1,0:T(8,128)} %copy-done.3, f32[1152]{0:T(1024)S(1)} %get-tuple-element.25, f32[1152]{0:T(1024)S(1)} %get-tuple-element.26, ...), kind=kOutput, calls=%fused_computation.53 | convolution fusion | flops 4768727040 | bytes 13726208 | tf_op jit(solution)/shard_map/dot_general | solution.py:105
  856.4 37.5 %all-reduce.14.cloned.1.call-done = bf16[1,448,1152]{2,1,0:T(8,128)(2,1)} async-done(((bf16[1,448,1152]{2,1,0:T(8,128)(2,1)}), bf16[1,448,1152]{2,1,0:T(8,128)(2,1)}) %all-reduce.14.cloned.1.call-update) | async-done | bytes 1032208 | tf_op jit(solution)/shard_map/psum | solution.py:160
  893.9 1.4 fusion.111
  895.3 1.4 multiply_reduce_fusion.4
  897.0 0.8 collective-permute-start
  901.8 0.7 add_select_fusion
  (93 shorter events, 8.8 us)
Async XLA Ops:
  7.2 41.5 %copy-start = (f32[16,1152]{1,0:T(8,128)S(1)}, f32[16,1152]{1,0:T(8,128)}, u32[]{:S(2)}) copy-start(f32[16,1152]{1,0:T(8,128)} %param.18) | copy-start | bytes 221188
  7.2 110.1 %all-reduce.16.cloned.1.call-start = ((), (), s32[]{:S(2)}) async-start(), calls=%async_computation.12 | async-start | bytes 516096
  35.6 3.3 copy-start.10
  38.8 3.1 copy-start.8
  41.9 151.1 %all-gather.16.cloned.1.call-start = ((), (), s32[]{:S(2)}) async-start(), calls=%async_computation | async-start | bytes 4644864 | tf_op jit(solution)/shard_map/all_gather | solution.py:100
  42.0 1.7 copy-start.11
  43.7 5.0 copy-start.12
  43.7 194.1 %all-gather.20.cloned.1.call-start = ((), (), s32[]{:S(2)}) async-start(), calls=%async_computation.6 | async-start | bytes 1658880 | tf_op jit(solution)/shard_map/all_gather | solution.py:107
  44.5 235.6 %all-reduce.8.cloned.1.call-start = ((), (), s32[]{:S(2)}) async-start(), calls=%async_computation.1 | async-start | bytes 2064384 | tf_op jit(solution)/shard_map/psum | solution.py:150
  50.8 142.1 %copy-start.2 = (f32[448,1152]{1,0:T(8,128)}, f32[448,1152]{1,0:T(8,128)S(1)}, u32[]{:S(2)}) copy-start(f32[448,1152]{1,0:T(8,128)S(1)} %get-tuple-element.59) | copy-start | bytes 6193156
  50.8 1.1 copy-start.14
  237.8 3.6 copy-start.6
  241.3 1.8 copy-start.7
  241.3 127.3 %all-gather.22.cloned.1.call-start = ((), (), s32[]{:S(2)}) async-start(), calls=%async_computation.7 | async-start | bytes 5971968 | tf_op jit(solution)/shard_map/all_gather | solution.py:100
  242.6 213.6 %all-gather.24.cloned.1.call-start = ((), (), s32[]{:S(2)}) async-start(), calls=%async_computation.8 | async-start | bytes 5971968 | tf_op jit(solution)/shard_map/all_gather | solution.py:107
  244.3 261.7 %all-reduce.10.cloned.1.call-start = ((), (), s32[]{:S(2)}) async-start(), calls=%async_computation.2 | async-start | bytes 2064384 | tf_op jit(solution)/shard_map/psum | solution.py:160
  467.1 112.7 %all-gather.18.cloned.1.call-start = ((), (), s32[]{:S(2)}) async-start(), calls=%async_computation.3 | async-start | bytes 4644864 | tf_op jit(solution)/shard_map/all_gather | solution.py:100
  468.7 156.0 %all-gather.26.cloned.1.call-start = ((), (), s32[]{:S(2)}) async-start(), calls=%async_computation.9 | async-start | bytes 1658880 | tf_op jit(solution)/shard_map/all_gather | solution.py:107
  469.5 197.7 %all-reduce.12.cloned.1.call-start = ((), (), s32[]{:S(2)}) async-start(), calls=%async_computation.4 | async-start | bytes 2064384 | tf_op jit(solution)/shard_map/psum | solution.py:150
  506.0 1.7 copy-start.5
  628.3 127.5 %all-gather.28.cloned.1.call-start = ((), (), s32[]{:S(2)}) async-start(), calls=%async_computation.10 | async-start | bytes 5971968 | tf_op jit(solution)/shard_map/all_gather | solution.py:100
  629.1 214.3 %all-gather.30.cloned.1.call-start = ((), (), s32[]{:S(2)}) async-start(), calls=%async_computation.11 | async-start | bytes 5971968 | tf_op jit(solution)/shard_map/all_gather | solution.py:107
  629.6 264.3 %all-reduce.14.cloned.1.call-start = ((), (), s32[]{:S(2)}) async-start(), calls=%async_computation.5 | async-start | bytes 2064384 | tf_op jit(solution)/shard_map/psum | solution.py:160
  668.9 1.3 copy-start.3
  843.4 50.6 %copy-start.4 = (f32[1,448,1152]{2,1,0:T(8,128)S(1)}, f32[1,448,1152]{2,1,0:T(8,128)}, u32[]{:S(2)}) copy-start(f32[1,448,1152]{2,1,0:T(8,128)} %copy-done.3) | copy-start | bytes 6193156
  855.0 41.6 %copy-start.13 = (bf16[1152,16]{0,1:T(8,128)(2,1)S(1)}, bf16[1152,16]{0,1:T(8,128)(2,1)}, u32[]{:S(2)}) copy-start(bf16[1152,16]{0,1:T(8,128)(2,1)} %param.25) | copy-start | bytes 110596
  893.9 2.7 copy-start.9
  893.9 8.6 copy-start.1
  897.0 4.8 collective-permute-start
Sparse Core Ops, SparseCore 0:
  42.0 75.2 all-reduce.15
  119.7 73.1 all-gather.15
  195.3 42.4 all-gather.19
  241.5 38.6 all-reduce.7
  282.4 86.2 all-gather.21
  370.9 85.2 all-gather.23
  467.2 38.7 all-reduce.9
  508.4 71.3 all-gather.17
  582.2 42.4 all-gather.25
  628.4 38.6 all-reduce.11
  669.6 86.2 all-gather.27
  758.1 85.2 all-gather.29
  855.2 38.7 all-reduce.13
where the time goes:
time: 917 us; the launch traced here: 909 us
  waiting for transfers between devices  686 us (75%)
  other arithmetic  78.8 us (9%)
  matrix products  68.4 us (7%)
  blocking collectives  32.2 us (4%)
  local copies, waits for them, and re-layouts  23.4 us (3%)
  between operations  19.1 us (2%)
    all_gather x4, waiting for transfers between devices, rows_product(): lax.all_gather(shard, 'batch', axis=0, tiled=True)  248 us
    all_gather x4, waiting for transfers between devices, cols_product(): lax.all_gather(shard, 'batch', axis=1, tiled=True)  224 us
    psum x4, waiting for transfers between devices, local(): branch = lax.psum(branch.astype(jnp.bfloat16), 'tensor').astype(jnp.float32)  147 us
    unnamed x14, waiting for transfers between devices  66.8 us
    slice x1, other arithmetic, local(): hidden_state = hidden_state + modulation[:, 5][:, None, :] * branch  62 us
    dot_general x4, matrix products, cols_product(): jnp.dot(activation, lax.all_gather(shard, 'batch', axis=1, tiled=True), p...  29.7 us
    all_gather x1, blocking collectives, local(): cond_all = lax.all_gather(cond_act, 'batch', axis=0, tiled=True)  25.4 us
  transfers between devices with their start and end apart: 14, of which 13 were waited for; matrix products, arithmetic and copies ran while one was open for 14% of the time, Pallas kernels for 0%

commit v1 on v0

--- a/solution.py
+++ b/solution.py
@@ -157,7 +157,10 @@
         branch = cols_product(hidden_units, down_weight[layer_at]).reshape(
             req_local, max_len, width
         )
-        branch = lax.psum(branch.astype(jnp.bfloat16), "tensor").astype(jnp.float32)
+        prepare_the_slabs = lambda matrix, lane_axis: jnp.sum(
+            lax.all_gather(matrix, lane_axis), axis=0
+        )
+        branch = prepare_the_slabs(branch.astype(jnp.bfloat16), "tensor").astype(jnp.float32)
         hidden_state = hidden_state + modulation[:, 5][:, None, :] * branch
     hidden_state = lax.dynamic_slice_in_dim(hidden_state, own_start, rows_local, 1)
     final_in = modulate(

time: 917 us -> 903 us (0.985)
  waiting for transfers between devices: 686 us -> 666 us
    psum x4 -> x2, waiting for transfers between devices: 147 us -> 72.1 us  [local(): branch = lax.psum(branch.astype(jnp.bfloat16), 'tensor').astype(jnp.float32)]
    all_gather x0 -> x2, waiting for transfers between devices: none -> 56.9 us  [local(): lax.all_gather(matrix, lane_axis)]
  transfers between devices with their start and end apart: 14 -> 14, of which waited for: 13 -> 13; matrix products, arithmetic and copies ran while one was open for 14% -> 15% of each run, Pallas kernels for 0% -> 0%
where the time goes in v1:
time: 903 us; the launch traced here: 896 us
  waiting for transfers between devices  666 us (74%)
  other arithmetic  82.2 us (9%)
  matrix products  67 us (7%)
  blocking collectives  32.2 us (4%)
  local copies, waits for them, and re-layouts  26.8 us (3%)
  between operations  19.3 us (2%)
    all_gather x4, waiting for transfers between devices, rows_product(): lax.all_gather(shard, 'batch', axis=0, tiled=True)  244 us
    all_gather x4, waiting for transfers between devices, cols_product(): lax.all_gather(shard, 'batch', axis=1, tiled=True)  227 us
    psum x2, waiting for transfers between devices, local(): branch = lax.psum(branch.astype(jnp.bfloat16), 'tensor').astype(jnp.float32)  72.1 us
    unnamed x14, waiting for transfers between devices  66.1 us
    slice x1, other arithmetic, local(): hidden_state = hidden_state + modulation[:, 5][:, None, :] * branch  62 us
    all_gather x2, waiting for transfers between devices, local(): lax.all_gather(matrix, lane_axis)  56.9 us
    dot_general x4, matrix products, cols_product(): jnp.dot(activation, lax.all_gather(shard, 'batch', axis=1, tiled=True), p...  29.1 us
    all_gather x1, blocking collectives, local(): cond_all = lax.all_gather(cond_act, 'batch', axis=0, tiled=True)  25.4 us
  transfers between devices with their start and end apart: 14, of which 13 were waited for; matrix products, arithmetic and copies ran while one was open for 15% of the time, Pallas kernels for 0%

profile of v1, /device:TPU:1, one launch (start us, length us, event | category | flops | bytes accessed | tf_op | source)
XLA Modules:
  0.0 895.6 jit_solution(7073533034282829304)
XLA Ops:
  7.9 25.4 %all-gather.8 = bf16[8,1,1152]{2,1,0:T(2,128)(2,1)S(1)} all-gather(bf16[1,1,1152]{2,1,0:T(2,128)(2,1)S(1)} %fusion.114), channel_id=1, replica_groups=mesh['guide'=2,'tensor'=2,'batch'=8] {'batch'}, dimensions={0}, use_global_device_ids=true | all-gather | bytes 20736 | tf_op jit(solution)/shard_map/all_gather | solution.py:112
  33.3 2.2 copy.40
  35.6 3.2 reshape.418
  39.2 2.7 fusion.52
  41.9 0.9 fusion.139
  43.1 1.3 reshape_squeeze.6
  44.5 0.8 fusion.140
  45.4 4.1 multiply_sine_fusion
  49.4 2.1 fusion.141
  53.2 64.1 %all-reduce.10.cloned.1.call-done = f32[8,8064]{1,0:T(8,128)} async-done(((f32[8,8064]{1,0:T(8,128)}), f32[8,8064]{1,0:T(8,128)}) %all-reduce.10.cloned.1.call-update) | async-done | bytes 258064
  117.3 1.7 dynamic-slice_reduce_fusion
  119.2 6.8 all_gather.43
  126.0 62.0 %slice_reduce_fusion.2 = (f32[1152]{0:T(1024)S(1)}, f32[1152]{0:T(1024)S(1)}, f32[1152]{0:T(1024)S(1)}, f32[1152]{0:T(1024)S(1)}, f32[1152]{0:T(1024)S(1)}, /*in...) fusion(f32[1,14,1152]{1,0,2:T(1,128)S(1)} %all_gather.43), kind=kLoop, calls=%fused_computation.104 | loop fusion | flops 5760 | bytes 129024 | tf_op jit(solution)/shard_map/slice | solution.py:164
  188.0 4.9 all-gather.20.cloned.1.call-done
  192.9 5.8 convolution_convert_fusion.1
  198.7 3.9 copy.43
  202.6 7.2 fusion.142
  209.7 4.9 fusion.60
  214.6 23.1 %all-gather.24.cloned.1.call-done = bf16[1,576,1152]{1,2,0:T(8,128)(2,1)} async-done(((bf16[1,576,144]{1,2,0:T(8,128)(2,1)}), bf16[1,576,1152]{1,2,0:T(8,128)(2,1)}) %all-gather.24.cloned.1.call-update) | async-done | bytes 1327120 | tf_op jit(solution)/shard_map/all_gather | solution.py:107
  237.8 3.7 fusion.50
  241.6 1.2 fusion.137
  242.8 2.5 fusion.138
  245.4 34.9 %all-reduce.6.cloned.1.call-done = bf16[1,448,1152]{2,1,0:T(8,128)(2,1)} async-done(((bf16[1,448,1152]{2,1,0:T(8,128)(2,1)}), bf16[1,448,1152]{2,1,0:T(8,128)(2,1)}) %all-reduce.6.cloned.1.call-update) | async-done | bytes 1032208 | tf_op jit(solution)/shard_map/psum | solution.py:150
  280.3 1.7 fusion.132
  282.5 86.3 %all-gather.26.cloned.1.call-done = bf16[1,1152,2304]{2,1,0:T(8,128)(2,1)} async-done(((bf16[1,144,2304]{2,1,0:T(8,128)(2,1)}), bf16[1,1152,2304]{2,1,0:T(8,128)(2,1)}) %all-gather.26.cloned.1.call-update) | async-done | bytes 5308432 | tf_op jit(solution)/shard_map/all_gather | solution.py:100
  368.8 87.5 %all-gather.28.cloned.1.call-done = bf16[1,2304,1152]{1,2,0:T(8,128)(2,1)} async-done(((bf16[1,2304,144]{1,2,0:T(8,128)(2,1)}), bf16[1,2304,1152]{1,2,0:T(8,128)(2,1)}) %all-gather.28.cloned.1.call-update) | async-done | bytes 5308432 | tf_op jit(solution)/shard_map/all_gather | solution.py:107
  456.4 11.1 %fusion.44 = bf16[448,1152]{1,0:T(8,128)(2,1)} fusion(bf16[1,2304,1152]{1,2,0:T(8,128)(2,1)} %all-gather.28.cloned.1.call-done, bf16[1,1152,2304]{2,1,0:T(8,128)(2,1)} %all-gather.26.cloned.1.call-done, f32[1152]{0:T(1024)S(1)} %get-tuple-element.34, f32[1152]{0:T(1024)S(1)} %get-tuple-element.35, f32[448]{0:T(512)S(1)} %add_rsqrt_fusion.2, ...), kind=kOutput, calls=%fused_computation.47 | convolution fusion | flops 4770275328 | bytes 14763008 | tf_op jit(solution)/shard_map/dot_general | solution.py:105
  467.5 2.2 copy.45
  469.8 2.4 reshape_squeeze.7
  473.2 26.3 %all-gather.30.cloned.1.call-done = bf16[896,1152]{1,0:T(8,128)(2,1)} async-done(((bf16[448,1152]{1,0:T(8,128)(2,1)}), bf16[896,1152]{1,0:T(8,128)(2,1)}) %all-gather.30.cloned.1.call-update) | async-done | bytes 2064400 | tf_op jit(solution)/shard_map/all_gather | solution.py:161
  499.4 3.2 reduce.20
  502.6 1.8 fusion.135
  504.5 1.3 copy-done.2
  506.1 67.2 %all-gather.22.cloned.1.call-done = bf16[1152,1728]{1,0:T(8,128)(2,1)} async-done(((bf16[144,1728]{1,0:T(8,128)(2,1)}), bf16[1152,1728]{1,0:T(8,128)(2,1)}) %all-gather.22.cloned.1.call-update) | async-done | bytes 3981328 | tf_op jit(solution)/shard_map/all_gather | solution.py:100
  573.3 5.1 convolution_convert_fusion
  578.4 1.4 copy.46
  579.8 5.9 fusion.143
  585.8 3.9 fusion.59
  589.7 28.5 %all-gather.32.cloned.1.call-done = bf16[1,576,1152]{1,2,0:T(8,128)(2,1)} async-done(((bf16[1,576,144]{1,2,0:T(8,128)(2,1)}), bf16[1,576,1152]{1,2,0:T(8,128)(2,1)}) %all-gather.32.cloned.1.call-update) | async-done | bytes 1327120 | tf_op jit(solution)/shard_map/all_gather | solution.py:107
  618.1 3.4 fusion.51
  623.2 37.2 %all-reduce.8.cloned.1.call-done = bf16[1,448,1152]{2,1,0:T(8,128)(2,1)} async-done(((bf16[1,448,1152]{2,1,0:T(8,128)(2,1)}), bf16[1,448,1152]{2,1,0:T(8,128)(2,1)}) %all-reduce.8.cloned.1.call-update) | async-done | bytes 1032208 | tf_op jit(solution)/shard_map/psum | solution.py:150
  660.4 2.2 fusion.134
  663.0 86.1 %all-gather.34.cloned.1.call-done = bf16[1,1152,2304]{2,1,0:T(8,128)(2,1)} async-done(((bf16[1,144,2304]{2,1,0:T(8,128)(2,1)}), bf16[1,1152,2304]{2,1,0:T(8,128)(2,1)}) %all-gather.34.cloned.1.call-update) | async-done | bytes 5308432 | tf_op jit(solution)/shard_map/all_gather | solution.py:100
  749.1 87.5 %all-gather.36.cloned.1.call-done = bf16[1,2304,1152]{1,2,0:T(8,128)(2,1)} async-done(((bf16[1,2304,144]{1,2,0:T(8,128)(2,1)}), bf16[1,2304,1152]{1,2,0:T(8,128)(2,1)}) %all-gather.36.cloned.1.call-update) | async-done | bytes 5308432 | tf_op jit(solution)/shard_map/all_gather | solution.py:107
  836.6 10.9 %fusion.47 = bf16[448,1152]{1,0:T(8,128)(2,1)} fusion(bf16[1,2304,1152]{1,2,0:T(8,128)(2,1)} %all-gather.36.cloned.1.call-done, bf16[1,1152,2304]{2,1,0:T(8,128)(2,1)} %all-gather.34.cloned.1.call-done, f32[1,448,1152]{2,1,0:T(8,128)S(1)} %get-tuple-element.45, f32[1152]{0:T(1024)S(1)} %get-tuple-element.25, f32[1152]{0:T(1024)S(1)} %get-tuple-element.26, ...), kind=kOutput, calls=%fused_computation.48 | convolution fusion | flops 4768727040 | bytes 13726208 | tf_op jit(solution)/shard_map/dot_general | solution.py:105
  848.9 30.6 %all-gather.38.cloned.1.call-done = bf16[896,1152]{1,0:T(8,128)(2,1)} async-done(((bf16[448,1152]{1,0:T(8,128)(2,1)}), bf16[896,1152]{1,0:T(8,128)(2,1)}) %all-gather.38.cloned.1.call-update) | async-done | bytes 2064400 | tf_op jit(solution)/shard_map/all_gather | solution.py:161
  879.5 2.5 reduce.21
  883.1 0.8 collective-permute-start
  (87 shorter events, 10.1 us)
Async XLA Ops:
  7.2 42.3 %copy-start = (f32[16,1152]{1,0:T(8,128)S(1)}, f32[16,1152]{1,0:T(8,128)}, u32[]{:S(2)}) copy-start(f32[16,1152]{1,0:T(8,128)} %param.18) | copy-start | bytes 221188
  7.2 110.1 %all-reduce.10.cloned.1.call-start = ((), (), s32[]{:S(2)}) async-start(), calls=%async_computation.12 | async-start | bytes 516096
  35.6 3.3 copy-start.6
  38.8 3.1 copy-start.5
  41.9 151.1 %all-gather.20.cloned.1.call-start = ((), (), s32[]{:S(2)}) async-start(), calls=%async_computation | async-start | bytes 4644864 | tf_op jit(solution)/shard_map/all_gather | solution.py:100
  42.8 1.7 copy-start.7
  44.4 5.0 copy-start.8
  44.4 193.3 %all-gather.24.cloned.1.call-start = ((), (), s32[]{:S(2)}) async-start(), calls=%async_computation.4 | async-start | bytes 1658880 | tf_op jit(solution)/shard_map/all_gather | solution.py:107
  45.3 235.0 %all-reduce.6.cloned.1.call-start = ((), (), s32[]{:S(2)}) async-start(), calls=%async_computation.1 | async-start | bytes 2064384 | tf_op jit(solution)/shard_map/psum | solution.py:150
  51.5 1.1 copy-start.10
  237.8 3.8 copy-start.4
  241.5 127.3 %all-gather.26.cloned.1.call-start = ((), (), s32[]{:S(2)}) async-start(), calls=%async_computation.5 | async-start | bytes 5971968 | tf_op jit(solution)/shard_map/all_gather | solution.py:100
  242.8 213.6 %all-gather.28.cloned.1.call-start = ((), (), s32[]{:S(2)}) async-start(), calls=%async_computation.6 | async-start | bytes 5971968 | tf_op jit(solution)/shard_map/all_gather | solution.py:107
  245.3 254.1 %all-gather.30.cloned.1.call-start = ((), (), s32[]{:S(2)}) async-start(), calls=%async_computation.7 | async-start | bytes 3096576 | tf_op jit(solution)/shard_map/all_gather | solution.py:161
  280.3 1.7 copy-start.3
  467.5 105.8 %all-gather.22.cloned.1.call-start = ((), (), s32[]{:S(2)}) async-start(), calls=%async_computation.2 | async-start | bytes 4644864 | tf_op jit(solution)/shard_map/all_gather | solution.py:100
  472.2 146.0 %all-gather.32.cloned.1.call-start = ((), (), s32[]{:S(2)}) async-start(), calls=%async_computation.8 | async-start | bytes 1658880 | tf_op jit(solution)/shard_map/all_gather | solution.py:107
  472.9 187.5 %all-reduce.8.cloned.1.call-start = ((), (), s32[]{:S(2)}) async-start(), calls=%async_computation.3 | async-start | bytes 2064384 | tf_op jit(solution)/shard_map/psum | solution.py:150
  504.4 1.3 copy-start.2
  621.6 127.5 %all-gather.34.cloned.1.call-start = ((), (), s32[]{:S(2)}) async-start(), calls=%async_computation.9 | async-start | bytes 5971968 | tf_op jit(solution)/shard_map/all_gather | solution.py:100
  622.3 214.3 %all-gather.36.cloned.1.call-start = ((), (), s32[]{:S(2)}) async-start(), calls=%async_computation.10 | async-start | bytes 5971968 | tf_op jit(solution)/shard_map/all_gather | solution.py:107
  622.9 256.6 %all-gather.38.cloned.1.call-start = ((), (), s32[]{:S(2)}) async-start(), calls=%async_computation.11 | async-start | bytes 3096576 | tf_op jit(solution)/shard_map/all_gather | solution.py:161
  882.0 0.8 copy-start.9
  882.0 6.6 copy-start.1
  883.1 4.8 collective-permute-start
Sparse Core Ops, SparseCore 0:
  42.0 75.2 all-reduce.9
  119.7 73.1 all-gather.19
  195.3 42.4 all-gather.23
  241.6 38.6 all-reduce.5
  282.6 86.2 all-gather.25
  371.1 85.2 all-gather.27
  467.6 31.7 all-gather.29
  501.9 71.3 all-gather.21
  575.7 42.4 all-gather.31
  621.7 38.6 all-reduce.7
  662.8 86.2 all-gather.33
  751.3 85.2 all-gather.35
  847.7 31.7 all-gather.37
